TPU v7x, 128 devices: a whole 4x4x4 slice. The times are simulated.
128 devices in a mesh: ocean: 2 (over core), ice: 64 (over z, y, x).
Axes of the slice: x: 4, y: 4, z: 4, core: 2. Of those that a mesh axis runs over, the one named last changes fastest.
Arguments:
- velocity: float32 [128, 512, 128], P('ocean', 'ice'), may hold values from -6 to 6
- stress: float32 [128, 512, 128], P('ocean', 'ice'), may hold values from -6 to 6
- thickness: float32 [128, 512, 128], P('ocean', 'ice'), may hold values from 0.5 to 2
- forcing: float32 [128, 512, 128], P('ocean', 'ice'), may hold values from -6 to 6
- switch: int32 [128, 512, 128], P('ocean', 'ice'), may hold values 0 or 1
- covered: int32 [128], P('ocean'), may hold values from 0 to 1, as said below
- reinit: int32 [128], P('ocean'), may hold values 0 or 1
- cot_velocity: float32 [128, 512, 128], P('ocean', 'ice'), may hold values from -6 to 6
- cot_stress: float32 [128, 512, 128], P('ocean', 'ice'), may hold values from -6 to 6
- kernel: float32 [512, 512], replicated, may hold values from 0 to 1, as said below
Outputs:
- grad_velocity: float32 [128, 512, 128], P('ocean', 'ice')
- grad_stress: float32 [128, 512, 128], P('ocean', 'ice')
- grad_thickness: float32 [128, 512, 128], P('ocean', 'ice')
- grad_forcing: float32 [128, 512, 128], P('ocean', 'ice')
Inputs may be any that keep to these rules, and one draw needn't show every extreme that they name: Exactly 32 blocks are covered; one index of ocean holds 31 of them and the other holds one. The kernel's diagonal exceeds the sum of each row's other entries.
All inputs are finite; a program needn't handle non-finite values. No bound on the sum of `switch` or of `reinit` on one device may be relied on, other than what follows from the above.
Results may differ from a plain program's by a relative error of at most 0.00015.
Values sent between devices are 32-bit elements; how exact they have to be, the bound alone decides.
No kernel may reach another device: no remote copies, remote signals or barrier semaphores. Data moves between devices by JAX's collectives and lax.ppermute only.
A program may use at most 64 MiB of HBM per device.

v0:
```python
import jax
import jax.numpy as jnp
from jax import lax
from jax.sharding import PartitionSpec as P

SUB = 8
WINDOWS = 2
PLASTIC = 0.25
VISCOUS = 1.0
GAMMA = 0.6
BETA = 0.9
STEP = 0.04


def passed_along(block, axis, distance):
    devices = range(lax.axis_size(axis))
    route = [(i - distance, i) for i in devices if i - distance in devices]
    return lax.ppermute(block, axis, route)


def prefix(part, axis, combine, identity):
    place = lax.axis_index(axis)
    gathered = lax.all_gather(part, axis)
    state = jnp.zeros_like(part) + jnp.asarray(identity, part.dtype)

    def one(turn, state):
        return combine(state, lax.dynamic_index_in_dim(gathered, turn, 0, False))

    return lax.fori_loop(0, place, one, state)


def forward_diff(x):
    above = passed_along(x[:, -1:], "ice", 1)
    upper = jnp.concatenate([above, x[:, :-1]], axis=1)
    left = jnp.pad(x, ((0, 0), (0, 0), (1, 0)))[:, :, :-1]
    return 2.0 * x - upper - left


def backward_diff(x):
    below = passed_along(x[:, :1], "ice", -1)
    lower = jnp.concatenate([x[:, 1:], below], axis=1)
    right = jnp.pad(x, ((0, 0), (0, 0), (0, 1)))[:, :, 1:]
    return 2.0 * x - lower - right


def ice_work(velo, stress_now, source, force, cot_u, cot_s, keep, kernel):
    rows_dev = velo.shape[1]
    first = lax.axis_index("ice") * rows_dev
    own_rows = lax.dynamic_slice_in_dim(kernel, first, rows_dev, 0)
    own_cols = lax.dynamic_slice_in_dim(kernel, first, rows_dev, 1)
    zeta = jnp.einsum(
        "ij,wjc->wic",
        own_rows,
        lax.all_gather(source, "ice", axis=1, tiled=True),
        precision=lax.Precision.HIGHEST,
    )
    scale = keep[:, None, None]

    def advance(carry, unused):
        u_now, s_now = carry
        strain = forward_diff(u_now)
        s_now = GAMMA * s_now + zeta * strain
        u_now = BETA * u_now - STEP * backward_diff(s_now) + STEP * force
        return ((u_now, s_now), strain)

    u_now, s_now = (velo, stress_now)
    strains = []
    for window in range(WINDOWS):
        if window > 0:
            s_now = s_now * scale
        (u_now, s_now), saved = lax.scan(advance, (u_now, s_now), None, length=SUB)
        strains.append(saved)

    def retreat(carry, strain):
        adj_u, adj_s, adj_z, adj_f = carry
        total_s = adj_s - STEP * forward_diff(adj_u)
        adj_f = adj_f + STEP * adj_u
        adj_u = BETA * adj_u + backward_diff(zeta * total_s)
        adj_z = adj_z + total_s * strain
        adj_s = GAMMA * total_s
        return ((adj_u, adj_s, adj_z, adj_f), None)

    zeros = jnp.zeros_like(velo)
    carry = (cot_u, cot_s, zeros, zeros)
    for window in range(WINDOWS - 1, -1, -1):
        carry, unused = lax.scan(retreat, carry, strains[window], reverse=True)
        if window > 0:
            carry = (carry[0], carry[1] * scale, carry[2], carry[3])
    adj_u, adj_s, adj_z, adj_f = carry
    adj_q = jnp.einsum(
        "ij,wic->wjc",
        own_cols,
        lax.all_gather(adj_z, "ice", axis=1, tiled=True),
        precision=lax.Precision.HIGHEST,
    )
    return (adj_u, adj_s, adj_q, adj_f)


def shards(
    velocity, stress, thickness, forcing, switch, covered, reinit, cot_velocity, cot_stress, kernel
):
    coef = jnp.where(switch == 1, PLASTIC, VISCOUS).astype(jnp.float32)
    source = thickness * coef
    keep = (1 - reinit).astype(jnp.float32)
    live = covered.astype(jnp.float32)[:, None, None]
    blocks = covered.shape[0]
    work = blocks // 4
    peers = lax.axis_size("ocean")
    cap = (min(blocks, work * peers) + peers - 1) // peers
    count = jnp.sum(covered)
    offset = prefix(count, "ocean", lambda early, late: early + late, jnp.int32(0))
    rank = jnp.cumsum(covered) - covered
    slot_ids = jnp.arange(peers * cap, dtype=jnp.int32)
    owner_of = slot_ids // cap
    place_of = slot_ids % cap
    wanted = place_of * peers + (owner_of - offset) % peers
    valid = wanted < count
    match = (covered[None, :] == 1) & (rank[None, :] == wanted[:, None])
    source_idx = jnp.sum(jnp.where(match, jnp.arange(blocks, dtype=jnp.int32)[None, :], 0), axis=1)
    work_slot = jnp.where(valid, (offset + wanted) // peers, -1).astype(jnp.float32)
    stacked = jnp.stack([velocity, stress, source, forcing, cot_velocity, cot_stress], axis=1)
    validf = valid.astype(jnp.float32)
    packed = jnp.take(stacked, source_idx, axis=0) * validf[:, None, None, None]
    keep_send = jnp.take(keep, source_idx, axis=0) * validf
    arrived, keep_recv, slot_recv = (
        lax.all_to_all(packed, "ocean", split_axis=0, concat_axis=0, tiled=True),
        lax.all_to_all(keep_send, "ocean", split_axis=0, concat_axis=0, tiled=True),
        lax.all_to_all(work_slot, "ocean", split_axis=0, concat_axis=0, tiled=True),
    )
    slot_int = slot_recv.astype(jnp.int32)
    picks = slot_int[None, :] == jnp.arange(work, dtype=jnp.int32)[:, None]
    pick_idx = jnp.sum(
        jnp.where(picks, jnp.arange(slot_int.shape[0], dtype=jnp.int32)[None, :], 0), axis=1
    )
    fields = jnp.take(arrived, pick_idx, axis=0)
    keep_work = jnp.take(keep_recv, pick_idx, axis=0)
    results = ice_work(
        fields[:, 0],
        fields[:, 1],
        fields[:, 2],
        fields[:, 3],
        fields[:, 4],
        fields[:, 5],
        keep_work,
        kernel,
    )
    gathered = jnp.stack(results, axis=1)
    present = (slot_int >= 0).astype(jnp.float32)
    outgoing = (
        jnp.take(gathered, jnp.clip(slot_int, 0, work - 1), axis=0) * present[:, None, None, None]
    )
    returned = lax.all_to_all(outgoing, "ocean", split_axis=0, concat_axis=0, tiled=True)
    global_idx = offset + rank
    home_slot = global_idx % peers * cap + rank // peers
    mine = jnp.take(returned, jnp.clip(home_slot, 0, peers * cap - 1), axis=0)
    grad_u, grad_s, grad_q, grad_f = (mine[:, 0], mine[:, 1], mine[:, 2], mine[:, 3])
    return (grad_u * live, grad_s * live, grad_q * coef * live, grad_f * live)


def solution(mesh):
    placed = (
        P("ocean", "ice", None),
        P("ocean", "ice", None),
        P("ocean", "ice", None),
        P("ocean", "ice", None),
        P("ocean", "ice", None),
        P("ocean"),
        P("ocean"),
        P("ocean", "ice", None),
        P("ocean", "ice", None),
        P(),
    )
    return jax.shard_map(
        shards,
        mesh=mesh,
        in_specs=placed,
        out_specs=(
            P("ocean", "ice", None),
            P("ocean", "ice", None),
            P("ocean", "ice", None),
            P("ocean", "ice", None),
        ),
        check_vma=False,
    )
```

profile of v0, /device:TPU:1, one launch (start us, length us, event | category | flops | bytes accessed | tf_op | source)
XLA Modules:
  0.0 721.2 jit_solution(8110284426354356338)
XLA Ops:
  45.0 77.3 %all-gather.6.cloned.1.call-done = f32[16,1,512,128]{3,2,0,1:T(8,128)} async-done(((f32[16,1,8,128]{3,2,0,1:T(8,128)}), f32[16,1,512,128]{3,2,0,1:T(8,128)}) %all-gather.6.cloned.1.call-update) | async-done | bytes 4194320 | tf_op jit(solution)/shard_map/all_gather | solution.py:54
  126.7 84.1 %while.84 = (s32[]{:T(128)}, f32[16,8,128]{2,1,0:T(8,128)S(1)}, f32[16,8,128]{2,1,0:T(8,128)S(1)}, f32[8,16,8,128]{3,2,1,0:T(8,128)S(1)}, f32[16,8,128]{2,1,0:T(...) while((s32[]{:T(128)}, f32[16,8,128]{2,1,0:T(8,128)S(1)}, f32[16,8,128]{2,1,0:T(8,128)S(1)}, ...), condition=%wide.region_7.8_spmd, body=%wide.region_6.7_spmd.sunk | while | flops 262146 | bytes 1073313 | solution.py:71
  154.7 5.5 collective-permute-start
  199.7 5.5 collective-permute-start
  211.0 90.0 %while.85 = (s32[]{:T(128)}, f32[16,8,128]{2,1,0:T(8,128)S(1)}, f32[16,8,128]{2,1,0:T(8,128)S(1)}, f32[8,16,8,128]{3,2,1,0:T(8,128)S(1)}, f32[16,8,128]{2,1,0:T(...) while((s32[]{:T(128)}, f32[16,8,128]{2,1,0:T(8,128)S(1)}, f32[16,8,128]{2,1,0:T(8,128)S(1)}, ...), condition=%wide.region_9.10_spmd, body=%wide.region_8.9_spmd.sunk | while | flops 262146 | bytes 1073313 | solution.py:71
  301.0 104.9 %while.87 = (s32[]{:T(128)}, f32[16,8,128]{2,1,0:T(8,128)S(1)}, f32[16,8,128]{2,1,0:T(8,128)S(1)}, f32[16,8,128]{2,1,0:T(8,128)S(1)}, f32[16,8,128]{2,1,0:T(8,12...) while((s32[]{:T(128)}, f32[16,8,128]{2,1,0:T(8,128)S(1)}, ...), condition=%wide.region_11.12_spmd.clone, body=%wide.region_10.11_spmd.clone.sunk | while | flops 327684 | bytes 1327311 | solution.py:86
  301.0 5.5 collective-permute-start.6
  312.8 7.3 %collective-permute-start.6 = (f32[16,1,128]{2,1,0:T(1,128)S(1)}, f32[16,1,128]{2,1,0:T(1,128)S(1)}, u32[]{:S(2)}, u32[]{:S(2)}) collective-permute-start(f32[16,1,128]{2,1,0:T(1,128)S(1)} %slice.355), channel_id=1, source_target_pairs={{0,1},{1,2},{2,3},{3,4},{4,5},{5,6},{6,7},{7,8},{8,9},{9,10},{10,1... | collective-permute-start | bytes 24584 | tf_op jit(solution)/shard_map/while/body/eval_jaxpr/ppermute | solution.py:18
  326.3 7.1 collective-permute-start.6
  339.0 7.8 %collective-permute-start.6 = (f32[16,1,128]{2,1,0:T(1,128)S(1)}, f32[16,1,128]{2,1,0:T(1,128)S(1)}, u32[]{:S(2)}, u32[]{:S(2)}) collective-permute-start(f32[16,1,128]{2,1,0:T(1,128)S(1)} %slice.355), channel_id=1, source_target_pairs={{0,1},{1,2},{2,3},{3,4},{4,5},{5,6},{6,7},{7,8},{8,9},{9,10},{10,1... | collective-permute-start | bytes 24584 | tf_op jit(solution)/shard_map/while/body/eval_jaxpr/ppermute | solution.py:18
  352.5 7.4 %collective-permute-start.6 = (f32[16,1,128]{2,1,0:T(1,128)S(1)}, f32[16,1,128]{2,1,0:T(1,128)S(1)}, u32[]{:S(2)}, u32[]{:S(2)}) collective-permute-start(f32[16,1,128]{2,1,0:T(1,128)S(1)} %slice.355), channel_id=1, source_target_pairs={{0,1},{1,2},{2,3},{3,4},{4,5},{5,6},{6,7},{7,8},{8,9},{9,10},{10,1... | collective-permute-start | bytes 24584 | tf_op jit(solution)/shard_map/while/body/eval_jaxpr/ppermute | solution.py:18
  365.8 7.6 %collective-permute-start.6 = (f32[16,1,128]{2,1,0:T(1,128)S(1)}, f32[16,1,128]{2,1,0:T(1,128)S(1)}, u32[]{:S(2)}, u32[]{:S(2)}) collective-permute-start(f32[16,1,128]{2,1,0:T(1,128)S(1)} %slice.355), channel_id=1, source_target_pairs={{0,1},{1,2},{2,3},{3,4},{4,5},{5,6},{6,7},{7,8},{8,9},{9,10},{10,1... | collective-permute-start | bytes 24584 | tf_op jit(solution)/shard_map/while/body/eval_jaxpr/ppermute | solution.py:18
  379.4 7.2 %collective-permute-start.6 = (f32[16,1,128]{2,1,0:T(1,128)S(1)}, f32[16,1,128]{2,1,0:T(1,128)S(1)}, u32[]{:S(2)}, u32[]{:S(2)}) collective-permute-start(f32[16,1,128]{2,1,0:T(1,128)S(1)} %slice.355), channel_id=1, source_target_pairs={{0,1},{1,2},{2,3},{3,4},{4,5},{5,6},{6,7},{7,8},{8,9},{9,10},{10,1... | collective-permute-start | bytes 24584 | tf_op jit(solution)/shard_map/while/body/eval_jaxpr/ppermute | solution.py:18
  392.6 7.3 %collective-permute-start.6 = (f32[16,1,128]{2,1,0:T(1,128)S(1)}, f32[16,1,128]{2,1,0:T(1,128)S(1)}, u32[]{:S(2)}, u32[]{:S(2)}) collective-permute-start(f32[16,1,128]{2,1,0:T(1,128)S(1)} %slice.355), channel_id=1, source_target_pairs={{0,1},{1,2},{2,3},{3,4},{4,5},{5,6},{6,7},{7,8},{8,9},{9,10},{10,1... | collective-permute-start | bytes 24584 | tf_op jit(solution)/shard_map/while/body/eval_jaxpr/ppermute | solution.py:18
  406.0 107.0 %while.86 = (s32[]{:T(128)}, f32[16,8,128]{2,1,0:T(8,128)S(1)}, f32[16,8,128]{2,1,0:T(8,128)S(1)}, f32[16,8,128]{2,1,0:T(8,128)S(1)}, f32[16,8,128]{2,1,0:T(8,12...) while((s32[]{:T(128)}, f32[16,8,128]{2,1,0:T(8,128)S(1)}, ...), condition=%wide.region_13.14_spmd, body=%wide.region_12.13_spmd.sunk | while | flops 294915 | bytes 1327293 | solution.py:86
  406.0 7.6 %collective-permute-start.4 = (f32[16,1,128]{2,1,0:T(1,128)S(1)}, f32[16,1,128]{2,1,0:T(1,128)S(1)}, u32[]{:S(2)}, u32[]{:S(2)}) collective-permute-start(f32[16,1,128]{2,1,0:T(1,128)S(1)} %slice.351), channel_id=1, source_target_pairs={{0,1},{1,2},{2,3},{3,4},{4,5},{5,6},{6,7},{7,8},{8,9},{9,10},{10,1... | collective-permute-start | bytes 24584 | tf_op jit(solution)/shard_map/while/body/eval_jaxpr/ppermute | solution.py:18
  419.5 7.3 %collective-permute-start.4 = (f32[16,1,128]{2,1,0:T(1,128)S(1)}, f32[16,1,128]{2,1,0:T(1,128)S(1)}, u32[]{:S(2)}, u32[]{:S(2)}) collective-permute-start(f32[16,1,128]{2,1,0:T(1,128)S(1)} %slice.351), channel_id=1, source_target_pairs={{0,1},{1,2},{2,3},{3,4},{4,5},{5,6},{6,7},{7,8},{8,9},{9,10},{10,1... | collective-permute-start | bytes 24584 | tf_op jit(solution)/shard_map/while/body/eval_jaxpr/ppermute | solution.py:18
  432.8 7.6 %collective-permute-start.4 = (f32[16,1,128]{2,1,0:T(1,128)S(1)}, f32[16,1,128]{2,1,0:T(1,128)S(1)}, u32[]{:S(2)}, u32[]{:S(2)}) collective-permute-start(f32[16,1,128]{2,1,0:T(1,128)S(1)} %slice.351), channel_id=1, source_target_pairs={{0,1},{1,2},{2,3},{3,4},{4,5},{5,6},{6,7},{7,8},{8,9},{9,10},{10,1... | collective-permute-start | bytes 24584 | tf_op jit(solution)/shard_map/while/body/eval_jaxpr/ppermute | solution.py:18
  446.1 7.3 %collective-permute-start.4 = (f32[16,1,128]{2,1,0:T(1,128)S(1)}, f32[16,1,128]{2,1,0:T(1,128)S(1)}, u32[]{:S(2)}, u32[]{:S(2)}) collective-permute-start(f32[16,1,128]{2,1,0:T(1,128)S(1)} %slice.351), channel_id=1, source_target_pairs={{0,1},{1,2},{2,3},{3,4},{4,5},{5,6},{6,7},{7,8},{8,9},{9,10},{10,1... | collective-permute-start | bytes 24584 | tf_op jit(solution)/shard_map/while/body/eval_jaxpr/ppermute | solution.py:18
  459.4 7.6 %collective-permute-start.4 = (f32[16,1,128]{2,1,0:T(1,128)S(1)}, f32[16,1,128]{2,1,0:T(1,128)S(1)}, u32[]{:S(2)}, u32[]{:S(2)}) collective-permute-start(f32[16,1,128]{2,1,0:T(1,128)S(1)} %slice.351), channel_id=1, source_target_pairs={{0,1},{1,2},{2,3},{3,4},{4,5},{5,6},{6,7},{7,8},{8,9},{9,10},{10,1... | collective-permute-start | bytes 24584 | tf_op jit(solution)/shard_map/while/body/eval_jaxpr/ppermute | solution.py:18
  473.0 7.2 collective-permute-start.4
  486.2 7.3 %collective-permute-start.4 = (f32[16,1,128]{2,1,0:T(1,128)S(1)}, f32[16,1,128]{2,1,0:T(1,128)S(1)}, u32[]{:S(2)}, u32[]{:S(2)}) collective-permute-start(f32[16,1,128]{2,1,0:T(1,128)S(1)} %slice.351), channel_id=1, source_target_pairs={{0,1},{1,2},{2,3},{3,4},{4,5},{5,6},{6,7},{7,8},{8,9},{9,10},{10,1... | collective-permute-start | bytes 24584 | tf_op jit(solution)/shard_map/while/body/eval_jaxpr/ppermute | solution.py:18
  500.0 7.0 collective-permute-start.4
  513.7 188.2 %all-gather.4.cloned.1.call-done = f32[16,512,128]{2,1,0:T(8,128)} async-done(((f32[16,8,128]{2,1,0:T(8,128)}), f32[16,512,128]{2,1,0:T(8,128)}) %all-gather.4.cloned.1.call-update) | async-done | bytes 4194320 | tf_op jit(solution)/shard_map/all_gather | solution.py:93
  (391 shorter events, 313.1 us)
Async XLA Ops:
  16.8 16.8 %all-to-all-start = ((f32[2,16,1]{1,2,0:T(1,128)}), f32[2,16,1]{1,2,0:T(1,128)S(1)}, u32[]{:S(2)}, u32[]{:S(2)}) async-start(f32[2,16,1]{1,2,0:T(1,128)} %bitcast.7), calls=%async_computation | async-start | bytes 2048 | tf_op jit(solution)/shard_map/all_to_all | solution.py:128
  41.6 80.7 %all-gather.6.cloned.1.call-start = ((), (), s32[]{:S(2)}) async-start(), calls=%async_computation.5 | async-start | bytes 4259840 | tf_op jit(solution)/shard_map/all_gather | solution.py:54
  44.9 657.0 %all-gather.4.cloned.1.call-start = ((), (), s32[]{:S(2)}) async-start(), calls=%async_computation.4 | async-start | bytes 4259840 | tf_op jit(solution)/shard_map/all_gather | solution.py:93
  154.7 6.3 collective-permute-start
  166.2 6.3 collective-permute-start
  177.3 6.3 collective-permute-start
  199.7 6.3 collective-permute-start
  278.4 6.3 collective-permute-start.2
  301.0 6.3 collective-permute-start.6
  312.8 8.1 %collective-permute-start.6 = (f32[16,1,128]{2,1,0:T(1,128)S(1)}, f32[16,1,128]{2,1,0:T(1,128)S(1)}, u32[]{:S(2)}, u32[]{:S(2)}) collective-permute-start(f32[16,1,128]{2,1,0:T(1,128)S(1)} %slice.355), channel_id=1, source_target_pairs={{0,1},{1,2},{2,3},{3,4},{4,5},{5,6},{6,7},{7,8},{8,9},{9,10},{10,1... | collective-permute-start | bytes 24584 | tf_op jit(solution)/shard_map/while/body/eval_jaxpr/ppermute | solution.py:18
  326.3 7.8 %collective-permute-start.6 = (f32[16,1,128]{2,1,0:T(1,128)S(1)}, f32[16,1,128]{2,1,0:T(1,128)S(1)}, u32[]{:S(2)}, u32[]{:S(2)}) collective-permute-start(f32[16,1,128]{2,1,0:T(1,128)S(1)} %slice.355), channel_id=1, source_target_pairs={{0,1},{1,2},{2,3},{3,4},{4,5},{5,6},{6,7},{7,8},{8,9},{9,10},{10,1... | collective-permute-start | bytes 24584 | tf_op jit(solution)/shard_map/while/body/eval_jaxpr/ppermute | solution.py:18
  339.0 8.6 %collective-permute-start.6 = (f32[16,1,128]{2,1,0:T(1,128)S(1)}, f32[16,1,128]{2,1,0:T(1,128)S(1)}, u32[]{:S(2)}, u32[]{:S(2)}) collective-permute-start(f32[16,1,128]{2,1,0:T(1,128)S(1)} %slice.355), channel_id=1, source_target_pairs={{0,1},{1,2},{2,3},{3,4},{4,5},{5,6},{6,7},{7,8},{8,9},{9,10},{10,1... | collective-permute-start | bytes 24584 | tf_op jit(solution)/shard_map/while/body/eval_jaxpr/ppermute | solution.py:18
  352.5 8.1 %collective-permute-start.6 = (f32[16,1,128]{2,1,0:T(1,128)S(1)}, f32[16,1,128]{2,1,0:T(1,128)S(1)}, u32[]{:S(2)}, u32[]{:S(2)}) collective-permute-start(f32[16,1,128]{2,1,0:T(1,128)S(1)} %slice.355), channel_id=1, source_target_pairs={{0,1},{1,2},{2,3},{3,4},{4,5},{5,6},{6,7},{7,8},{8,9},{9,10},{10,1... | collective-permute-start | bytes 24584 | tf_op jit(solution)/shard_map/while/body/eval_jaxpr/ppermute | solution.py:18
  365.8 8.4 %collective-permute-start.6 = (f32[16,1,128]{2,1,0:T(1,128)S(1)}, f32[16,1,128]{2,1,0:T(1,128)S(1)}, u32[]{:S(2)}, u32[]{:S(2)}) collective-permute-start(f32[16,1,128]{2,1,0:T(1,128)S(1)} %slice.355), channel_id=1, source_target_pairs={{0,1},{1,2},{2,3},{3,4},{4,5},{5,6},{6,7},{7,8},{8,9},{9,10},{10,1... | collective-permute-start | bytes 24584 | tf_op jit(solution)/shard_map/while/body/eval_jaxpr/ppermute | solution.py:18
  379.4 8.0 %collective-permute-start.6 = (f32[16,1,128]{2,1,0:T(1,128)S(1)}, f32[16,1,128]{2,1,0:T(1,128)S(1)}, u32[]{:S(2)}, u32[]{:S(2)}) collective-permute-start(f32[16,1,128]{2,1,0:T(1,128)S(1)} %slice.355), channel_id=1, source_target_pairs={{0,1},{1,2},{2,3},{3,4},{4,5},{5,6},{6,7},{7,8},{8,9},{9,10},{10,1... | collective-permute-start | bytes 24584 | tf_op jit(solution)/shard_map/while/body/eval_jaxpr/ppermute | solution.py:18
  392.6 8.0 %collective-permute-start.6 = (f32[16,1,128]{2,1,0:T(1,128)S(1)}, f32[16,1,128]{2,1,0:T(1,128)S(1)}, u32[]{:S(2)}, u32[]{:S(2)}) collective-permute-start(f32[16,1,128]{2,1,0:T(1,128)S(1)} %slice.355), channel_id=1, source_target_pairs={{0,1},{1,2},{2,3},{3,4},{4,5},{5,6},{6,7},{7,8},{8,9},{9,10},{10,1... | collective-permute-start | bytes 24584 | tf_op jit(solution)/shard_map/while/body/eval_jaxpr/ppermute | solution.py:18
  406.0 8.4 %collective-permute-start.4 = (f32[16,1,128]{2,1,0:T(1,128)S(1)}, f32[16,1,128]{2,1,0:T(1,128)S(1)}, u32[]{:S(2)}, u32[]{:S(2)}) collective-permute-start(f32[16,1,128]{2,1,0:T(1,128)S(1)} %slice.351), channel_id=1, source_target_pairs={{0,1},{1,2},{2,3},{3,4},{4,5},{5,6},{6,7},{7,8},{8,9},{9,10},{10,1... | collective-permute-start | bytes 24584 | tf_op jit(solution)/shard_map/while/body/eval_jaxpr/ppermute | solution.py:18
  419.5 8.1 %collective-permute-start.4 = (f32[16,1,128]{2,1,0:T(1,128)S(1)}, f32[16,1,128]{2,1,0:T(1,128)S(1)}, u32[]{:S(2)}, u32[]{:S(2)}) collective-permute-start(f32[16,1,128]{2,1,0:T(1,128)S(1)} %slice.351), channel_id=1, source_target_pairs={{0,1},{1,2},{2,3},{3,4},{4,5},{5,6},{6,7},{7,8},{8,9},{9,10},{10,1... | collective-permute-start | bytes 24584 | tf_op jit(solution)/shard_map/while/body/eval_jaxpr/ppermute | solution.py:18
  432.8 8.4 %collective-permute-start.4 = (f32[16,1,128]{2,1,0:T(1,128)S(1)}, f32[16,1,128]{2,1,0:T(1,128)S(1)}, u32[]{:S(2)}, u32[]{:S(2)}) collective-permute-start(f32[16,1,128]{2,1,0:T(1,128)S(1)} %slice.351), channel_id=1, source_target_pairs={{0,1},{1,2},{2,3},{3,4},{4,5},{5,6},{6,7},{7,8},{8,9},{9,10},{10,1... | collective-permute-start | bytes 24584 | tf_op jit(solution)/shard_map/while/body/eval_jaxpr/ppermute | solution.py:18
  446.1 8.1 %collective-permute-start.4 = (f32[16,1,128]{2,1,0:T(1,128)S(1)}, f32[16,1,128]{2,1,0:T(1,128)S(1)}, u32[]{:S(2)}, u32[]{:S(2)}) collective-permute-start(f32[16,1,128]{2,1,0:T(1,128)S(1)} %slice.351), channel_id=1, source_target_pairs={{0,1},{1,2},{2,3},{3,4},{4,5},{5,6},{6,7},{7,8},{8,9},{9,10},{10,1... | collective-permute-start | bytes 24584 | tf_op jit(solution)/shard_map/while/body/eval_jaxpr/ppermute | solution.py:18
  459.4 8.4 %collective-permute-start.4 = (f32[16,1,128]{2,1,0:T(1,128)S(1)}, f32[16,1,128]{2,1,0:T(1,128)S(1)}, u32[]{:S(2)}, u32[]{:S(2)}) collective-permute-start(f32[16,1,128]{2,1,0:T(1,128)S(1)} %slice.351), channel_id=1, source_target_pairs={{0,1},{1,2},{2,3},{3,4},{4,5},{5,6},{6,7},{7,8},{8,9},{9,10},{10,1... | collective-permute-start | bytes 24584 | tf_op jit(solution)/shard_map/while/body/eval_jaxpr/ppermute | solution.py:18
  473.0 8.0 %collective-permute-start.4 = (f32[16,1,128]{2,1,0:T(1,128)S(1)}, f32[16,1,128]{2,1,0:T(1,128)S(1)}, u32[]{:S(2)}, u32[]{:S(2)}) collective-permute-start(f32[16,1,128]{2,1,0:T(1,128)S(1)} %slice.351), channel_id=1, source_target_pairs={{0,1},{1,2},{2,3},{3,4},{4,5},{5,6},{6,7},{7,8},{8,9},{9,10},{10,1... | collective-permute-start | bytes 24584 | tf_op jit(solution)/shard_map/while/body/eval_jaxpr/ppermute | solution.py:18
  486.2 8.1 %collective-permute-start.4 = (f32[16,1,128]{2,1,0:T(1,128)S(1)}, f32[16,1,128]{2,1,0:T(1,128)S(1)}, u32[]{:S(2)}, u32[]{:S(2)}) collective-permute-start(f32[16,1,128]{2,1,0:T(1,128)S(1)} %slice.351), channel_id=1, source_target_pairs={{0,1},{1,2},{2,3},{3,4},{4,5},{5,6},{6,7},{7,8},{8,9},{9,10},{10,1... | collective-permute-start | bytes 24584 | tf_op jit(solution)/shard_map/while/body/eval_jaxpr/ppermute | solution.py:18
  500.0 7.8 %collective-permute-start.4 = (f32[16,1,128]{2,1,0:T(1,128)S(1)}, f32[16,1,128]{2,1,0:T(1,128)S(1)}, u32[]{:S(2)}, u32[]{:S(2)}) collective-permute-start(f32[16,1,128]{2,1,0:T(1,128)S(1)} %slice.351), channel_id=1, source_target_pairs={{0,1},{1,2},{2,3},{3,4},{4,5},{5,6},{6,7},{7,8},{8,9},{9,10},{10,1... | collective-permute-start | bytes 24584 | tf_op jit(solution)/shard_map/while/body/eval_jaxpr/ppermute | solution.py:18
  (52 other events, 436.5 us)
Sparse Core Ops, SparseCore 0:
  45.7 76.5 all-gather.5
  513.7 188.1 all-gather.3
where the time goes:
time: 724 us; the launch traced here: 721 us
  waiting for transfers between devices  403 us (56%)
  starting transfers between devices  248 us (34%)
  local copies, waits for them, and re-layouts  17.8 us (2%)
  other arithmetic  17.4 us (2%)
  between operations  14.4 us (2%)
  matrix products  8.86 us (1%)
  blocking collectives  8.21 us (1%)
    ppermute x64, starting transfers between devices, passed_along(): return lax.ppermute(block, axis, route)  238 us
    all_gather x1, waiting for transfers between devices, ice_work(): lax.all_gather(adj_z, 'ice', axis=1, tiled=True)  188 us
    ppermute x64, waiting for transfers between devices, passed_along(): return lax.ppermute(block, axis, route)  138 us
    all_gather x1, waiting for transfers between devices, ice_work(): lax.all_gather(source, 'ice', axis=1, tiled=True)  77.3 us
  transfers between devices with their start and end apart: 69, of which 66 were waited for; matrix products, arithmetic and copies ran while one was open for 2% of the time, Pallas kernels for 0%

commit v1 on v0

--- a/solution.py
+++ b/solution.py
@@ -10,6 +10,14 @@
 GAMMA = 0.6
 BETA = 0.9
 STEP = 0.04
+
+
+def tiled_gather(shard, axis, dim):
+    size = lax.axis_size(axis)
+    repeats = [size if d == dim else 1 for d in range(shard.ndim)]
+    return lax.all_to_all(
+        jnp.tile(shard, repeats), axis, split_axis=dim, concat_axis=dim, tiled=True
+    )
 
 
 def passed_along(block, axis, distance):
@@ -88,10 +96,7 @@
             carry = (carry[0], carry[1] * scale, carry[2], carry[3])
     adj_u, adj_s, adj_z, adj_f = carry
     adj_q = jnp.einsum(
-        "ij,wic->wjc",
-        own_cols,
-        lax.all_gather(adj_z, "ice", axis=1, tiled=True),
-        precision=lax.Precision.HIGHEST,
+        "ij,wic->wjc", own_cols, tiled_gather(adj_z, "ice", 1), precision=lax.Precision.HIGHEST
     )
     return (adj_u, adj_s, adj_q, adj_f)
 

time: 724 us -> 694 us (0.959)
  waiting for transfers between devices: 403 us -> 246 us
  blocking collectives: 8.21 us -> 82.5 us
  starting transfers between devices: 248 us -> 299 us
    all_gather x1 -> x0, waiting for transfers between devices: 188 us -> none  [ice_work(): lax.all_gather(adj_z, 'ice', axis=1, tiled=True)]
    all_to_all x1, blocking collectives: 5.32 us -> 79.6 us  [shards(): lax.all_to_all(outgoing, 'ocean', split_axis=0, concat_axis=0, tiled=True)]
    all_to_all x0 -> x1, starting transfers between devices: none -> 50.5 us  [tiled_gather(): lax.all_to_all(jnp.tile(shard, repeats), axis, split_axis=dim, concat_axi...]
    all_to_all x0 -> x1, waiting for transfers between devices: none -> 30.4 us  [tiled_gather(): lax.all_to_all(jnp.tile(shard, repeats), axis, split_axis=dim, concat_axi...]
where the time goes in v1:
time: 694 us; the launch traced here: 691 us
  starting transfers between devices  299 us (43%)
  waiting for transfers between devices  246 us (35%)
  blocking collectives  82.5 us (12%)
  local copies, waits for them, and re-layouts  19.7 us (3%)
  other arithmetic  17.5 us (3%)
  between operations  14.4 us (2%)
  matrix products  9.91 us (1%)
    ppermute x64, starting transfers between devices, passed_along(): return lax.ppermute(block, axis, route)  238 us
    ppermute x64, waiting for transfers between devices, passed_along(): return lax.ppermute(block, axis, route)  138 us
    all_to_all x1, blocking collectives, shards(): lax.all_to_all(outgoing, 'ocean', split_axis=0, concat_axis=0, tiled=True)  79.6 us
    all_gather x1, waiting for transfers between devices, ice_work(): lax.all_gather(source, 'ice', axis=1, tiled=True)  77.3 us
    all_to_all x1, starting transfers between devices, tiled_gather(): lax.all_to_all(jnp.tile(shard, repeats), axis, split_axis=dim, concat_axi...  50.5 us
    all_to_all x1, waiting for transfers between devices, tiled_gather(): lax.all_to_all(jnp.tile(shard, repeats), axis, split_axis=dim, concat_axi...  30.4 us
  transfers between devices with their start and end apart: 69, of which 66 were waited for; matrix products, arithmetic and copies ran while one was open for 2% of the time, Pallas kernels for 0%

profile of v1, /device:TPU:1, one launch (start us, length us, event | category | flops | bytes accessed | tf_op | source)
XLA Modules:
  0.0 691.2 jit_solution(13407873215545136583)
XLA Ops:
  45.0 77.3 %all-gather.3.cloned.1.call-done = f32[16,1,512,128]{3,2,0,1:T(8,128)} async-done(((f32[16,1,8,128]{3,2,0,1:T(8,128)}), f32[16,1,512,128]{3,2,0,1:T(8,128)}) %all-gather.3.cloned.1.call-update) | async-done | bytes 4194320 | tf_op jit(solution)/shard_map/all_gather | solution.py:62
  126.8 84.1 %while.84 = (s32[]{:T(128)}, f32[16,8,128]{2,1,0:T(8,128)S(1)}, f32[16,8,128]{2,1,0:T(8,128)S(1)}, f32[8,16,8,128]{3,2,1,0:T(8,128)S(1)}, f32[16,8,128]{2,1,0:T(...) while((s32[]{:T(128)}, f32[16,8,128]{2,1,0:T(8,128)S(1)}, f32[16,8,128]{2,1,0:T(8,128)S(1)}, ...), condition=%wide.region_7.8_spmd, body=%wide.region_6.7_spmd.sunk | while | flops 262146 | bytes 1073313 | solution.py:79
  211.1 90.0 %while.85 = (s32[]{:T(128)}, f32[16,8,128]{2,1,0:T(8,128)S(1)}, f32[16,8,128]{2,1,0:T(8,128)S(1)}, f32[8,16,8,128]{3,2,1,0:T(8,128)S(1)}, f32[16,8,128]{2,1,0:T(...) while((s32[]{:T(128)}, f32[16,8,128]{2,1,0:T(8,128)S(1)}, f32[16,8,128]{2,1,0:T(8,128)S(1)}, ...), condition=%wide.region_9.10_spmd, body=%wide.region_8.9_spmd.sunk | while | flops 262146 | bytes 1073313 | solution.py:79
  301.0 104.9 %while.87 = (s32[]{:T(128)}, f32[16,8,128]{2,1,0:T(8,128)S(1)}, f32[16,8,128]{2,1,0:T(8,128)S(1)}, f32[16,8,128]{2,1,0:T(8,128)S(1)}, f32[16,8,128]{2,1,0:T(8,12...) while((s32[]{:T(128)}, f32[16,8,128]{2,1,0:T(8,128)S(1)}, ...), condition=%wide.region_11.12_spmd.clone, body=%wide.region_10.11_spmd.clone.sunk | while | flops 327684 | bytes 1327311 | solution.py:94
  312.8 7.3 %collective-permute-start.6 = (f32[16,1,128]{2,1,0:T(1,128)S(1)}, f32[16,1,128]{2,1,0:T(1,128)S(1)}, u32[]{:S(2)}, u32[]{:S(2)}) collective-permute-start(f32[16,1,128]{2,1,0:T(1,128)S(1)} %slice.355), channel_id=1, source_target_pairs={{0,1},{1,2},{2,3},{3,4},{4,5},{5,6},{6,7},{7,8},{8,9},{9,10},{10,1... | collective-permute-start | bytes 24584 | tf_op jit(solution)/shard_map/while/body/eval_jaxpr/ppermute | solution.py:26
  326.3 7.1 %collective-permute-start.6 = (f32[16,1,128]{2,1,0:T(1,128)S(1)}, f32[16,1,128]{2,1,0:T(1,128)S(1)}, u32[]{:S(2)}, u32[]{:S(2)}) collective-permute-start(f32[16,1,128]{2,1,0:T(1,128)S(1)} %slice.355), channel_id=1, source_target_pairs={{0,1},{1,2},{2,3},{3,4},{4,5},{5,6},{6,7},{7,8},{8,9},{9,10},{10,1... | collective-permute-start | bytes 24584 | tf_op jit(solution)/shard_map/while/body/eval_jaxpr/ppermute | solution.py:26
  339.1 7.8 %collective-permute-start.6 = (f32[16,1,128]{2,1,0:T(1,128)S(1)}, f32[16,1,128]{2,1,0:T(1,128)S(1)}, u32[]{:S(2)}, u32[]{:S(2)}) collective-permute-start(f32[16,1,128]{2,1,0:T(1,128)S(1)} %slice.355), channel_id=1, source_target_pairs={{0,1},{1,2},{2,3},{3,4},{4,5},{5,6},{6,7},{7,8},{8,9},{9,10},{10,1... | collective-permute-start | bytes 24584 | tf_op jit(solution)/shard_map/while/body/eval_jaxpr/ppermute | solution.py:26
  352.6 7.4 %collective-permute-start.6 = (f32[16,1,128]{2,1,0:T(1,128)S(1)}, f32[16,1,128]{2,1,0:T(1,128)S(1)}, u32[]{:S(2)}, u32[]{:S(2)}) collective-permute-start(f32[16,1,128]{2,1,0:T(1,128)S(1)} %slice.355), channel_id=1, source_target_pairs={{0,1},{1,2},{2,3},{3,4},{4,5},{5,6},{6,7},{7,8},{8,9},{9,10},{10,1... | collective-permute-start | bytes 24584 | tf_op jit(solution)/shard_map/while/body/eval_jaxpr/ppermute | solution.py:26
  365.9 7.6 %collective-permute-start.6 = (f32[16,1,128]{2,1,0:T(1,128)S(1)}, f32[16,1,128]{2,1,0:T(1,128)S(1)}, u32[]{:S(2)}, u32[]{:S(2)}) collective-permute-start(f32[16,1,128]{2,1,0:T(1,128)S(1)} %slice.355), channel_id=1, source_target_pairs={{0,1},{1,2},{2,3},{3,4},{4,5},{5,6},{6,7},{7,8},{8,9},{9,10},{10,1... | collective-permute-start | bytes 24584 | tf_op jit(solution)/shard_map/while/body/eval_jaxpr/ppermute | solution.py:26
  379.5 7.2 %collective-permute-start.6 = (f32[16,1,128]{2,1,0:T(1,128)S(1)}, f32[16,1,128]{2,1,0:T(1,128)S(1)}, u32[]{:S(2)}, u32[]{:S(2)}) collective-permute-start(f32[16,1,128]{2,1,0:T(1,128)S(1)} %slice.355), channel_id=1, source_target_pairs={{0,1},{1,2},{2,3},{3,4},{4,5},{5,6},{6,7},{7,8},{8,9},{9,10},{10,1... | collective-permute-start | bytes 24584 | tf_op jit(solution)/shard_map/while/body/eval_jaxpr/ppermute | solution.py:26
  392.7 7.3 %collective-permute-start.6 = (f32[16,1,128]{2,1,0:T(1,128)S(1)}, f32[16,1,128]{2,1,0:T(1,128)S(1)}, u32[]{:S(2)}, u32[]{:S(2)}) collective-permute-start(f32[16,1,128]{2,1,0:T(1,128)S(1)} %slice.355), channel_id=1, source_target_pairs={{0,1},{1,2},{2,3},{3,4},{4,5},{5,6},{6,7},{7,8},{8,9},{9,10},{10,1... | collective-permute-start | bytes 24584 | tf_op jit(solution)/shard_map/while/body/eval_jaxpr/ppermute | solution.py:26
  406.0 107.0 %while.86 = (s32[]{:T(128)}, f32[16,8,128]{2,1,0:T(8,128)S(1)}, f32[16,8,128]{2,1,0:T(8,128)S(1)}, f32[16,8,128]{2,1,0:T(8,128)S(1)}, f32[16,8,128]{2,1,0:T(8,12...) while((s32[]{:T(128)}, f32[16,8,128]{2,1,0:T(8,128)S(1)}, ...), condition=%wide.region_13.14_spmd, body=%wide.region_12.13_spmd.sunk | while | flops 294915 | bytes 1327293 | solution.py:94
  406.0 7.6 %collective-permute-start.4 = (f32[16,1,128]{2,1,0:T(1,128)S(1)}, f32[16,1,128]{2,1,0:T(1,128)S(1)}, u32[]{:S(2)}, u32[]{:S(2)}) collective-permute-start(f32[16,1,128]{2,1,0:T(1,128)S(1)} %slice.351), channel_id=1, source_target_pairs={{0,1},{1,2},{2,3},{3,4},{4,5},{5,6},{6,7},{7,8},{8,9},{9,10},{10,1... | collective-permute-start | bytes 24584 | tf_op jit(solution)/shard_map/while/body/eval_jaxpr/ppermute | solution.py:26
  419.6 7.3 %collective-permute-start.4 = (f32[16,1,128]{2,1,0:T(1,128)S(1)}, f32[16,1,128]{2,1,0:T(1,128)S(1)}, u32[]{:S(2)}, u32[]{:S(2)}) collective-permute-start(f32[16,1,128]{2,1,0:T(1,128)S(1)} %slice.351), channel_id=1, source_target_pairs={{0,1},{1,2},{2,3},{3,4},{4,5},{5,6},{6,7},{7,8},{8,9},{9,10},{10,1... | collective-permute-start | bytes 24584 | tf_op jit(solution)/shard_map/while/body/eval_jaxpr/ppermute | solution.py:26
  432.8 7.6 %collective-permute-start.4 = (f32[16,1,128]{2,1,0:T(1,128)S(1)}, f32[16,1,128]{2,1,0:T(1,128)S(1)}, u32[]{:S(2)}, u32[]{:S(2)}) collective-permute-start(f32[16,1,128]{2,1,0:T(1,128)S(1)} %slice.351), channel_id=1, source_target_pairs={{0,1},{1,2},{2,3},{3,4},{4,5},{5,6},{6,7},{7,8},{8,9},{9,10},{10,1... | collective-permute-start | bytes 24584 | tf_op jit(solution)/shard_map/while/body/eval_jaxpr/ppermute | solution.py:26
  446.1 7.3 %collective-permute-start.4 = (f32[16,1,128]{2,1,0:T(1,128)S(1)}, f32[16,1,128]{2,1,0:T(1,128)S(1)}, u32[]{:S(2)}, u32[]{:S(2)}) collective-permute-start(f32[16,1,128]{2,1,0:T(1,128)S(1)} %slice.351), channel_id=1, source_target_pairs={{0,1},{1,2},{2,3},{3,4},{4,5},{5,6},{6,7},{7,8},{8,9},{9,10},{10,1... | collective-permute-start | bytes 24584 | tf_op jit(solution)/shard_map/while/body/eval_jaxpr/ppermute | solution.py:26
  459.4 7.6 %collective-permute-start.4 = (f32[16,1,128]{2,1,0:T(1,128)S(1)}, f32[16,1,128]{2,1,0:T(1,128)S(1)}, u32[]{:S(2)}, u32[]{:S(2)}) collective-permute-start(f32[16,1,128]{2,1,0:T(1,128)S(1)} %slice.351), channel_id=1, source_target_pairs={{0,1},{1,2},{2,3},{3,4},{4,5},{5,6},{6,7},{7,8},{8,9},{9,10},{10,1... | collective-permute-start | bytes 24584 | tf_op jit(solution)/shard_map/while/body/eval_jaxpr/ppermute | solution.py:26
  473.0 7.2 %collective-permute-start.4 = (f32[16,1,128]{2,1,0:T(1,128)S(1)}, f32[16,1,128]{2,1,0:T(1,128)S(1)}, u32[]{:S(2)}, u32[]{:S(2)}) collective-permute-start(f32[16,1,128]{2,1,0:T(1,128)S(1)} %slice.351), channel_id=1, source_target_pairs={{0,1},{1,2},{2,3},{3,4},{4,5},{5,6},{6,7},{7,8},{8,9},{9,10},{10,1... | collective-permute-start | bytes 24584 | tf_op jit(solution)/shard_map/while/body/eval_jaxpr/ppermute | solution.py:26
  486.2 7.3 %collective-permute-start.4 = (f32[16,1,128]{2,1,0:T(1,128)S(1)}, f32[16,1,128]{2,1,0:T(1,128)S(1)}, u32[]{:S(2)}, u32[]{:S(2)}) collective-permute-start(f32[16,1,128]{2,1,0:T(1,128)S(1)} %slice.351), channel_id=1, source_target_pairs={{0,1},{1,2},{2,3},{3,4},{4,5},{5,6},{6,7},{7,8},{8,9},{9,10},{10,1... | collective-permute-start | bytes 24584 | tf_op jit(solution)/shard_map/while/body/eval_jaxpr/ppermute | solution.py:26
  500.1 7.0 %collective-permute-start.4 = (f32[16,1,128]{2,1,0:T(1,128)S(1)}, f32[16,1,128]{2,1,0:T(1,128)S(1)}, u32[]{:S(2)}, u32[]{:S(2)}) collective-permute-start(f32[16,1,128]{2,1,0:T(1,128)S(1)} %slice.351), channel_id=1, source_target_pairs={{0,1},{1,2},{2,3},{3,4},{4,5},{5,6},{6,7},{7,8},{8,9},{9,10},{10,1... | collective-permute-start | bytes 24584 | tf_op jit(solution)/shard_map/while/body/eval_jaxpr/ppermute | solution.py:26
  515.5 50.5 %all-to-all-start.3 = ((f32[16,512,128]{2,0,1:T(8,128)}), f32[16,512,128]{2,0,1:T(8,128)}, u32[]{:S(2)}, u32[]{:S(2)}) async-start(f32[16,512,128]{2,0,1:T(8,128)} %bitcast.129), calls=%async_computation.3 | async-start | bytes 8388608 | tf_op jit(solution)/shard_map/all_to_all | solution.py:18
  566.1 30.4 %all-to-all-done.3 = f32[16,512,128]{2,0,1:T(8,128)} async-done(((f32[16,512,128]{2,0,1:T(8,128)}), f32[16,512,128]{2,0,1:T(8,128)}, u32[]{:S(2)}, u32[]{:S(2)}) %all-to-all-start.3) | async-done | bytes 4194336 | tf_op jit(solution)/shard_map/all_to_all | solution.py:18
  596.5 5.5 fusion.29
  602.8 79.6 %all_to_all.30 = f32[32,4,8,128]{3,2,1,0:T(8,128)S(1)} all-to-all(f32[32,4,8,128]{3,2,1,0:T(8,128)S(1)} %select_multiply_fusion.1), channel_id=1, replica_groups=mesh['ocean'=2,'ice'=64] {'ocean'}, dimensions={0} | all-to-all | bytes 1048576 | tf_op jit(solution)/shard_map/all_to_all | solution.py:157
  (390 shorter events, 321.7 us)
Async XLA Ops:
  16.8 16.8 %all-to-all-start = ((f32[2,16,1]{1,2,0:T(1,128)}), f32[2,16,1]{1,2,0:T(1,128)S(1)}, u32[]{:S(2)}, u32[]{:S(2)}) async-start(f32[2,16,1]{1,2,0:T(1,128)} %bitcast.7), calls=%async_computation | async-start | bytes 2048 | tf_op jit(solution)/shard_map/all_to_all | solution.py:133
  41.6 80.7 %all-gather.3.cloned.1.call-start = ((), (), s32[]{:S(2)}) async-start(), calls=%async_computation.5 | async-start | bytes 4259840 | tf_op jit(solution)/shard_map/all_gather | solution.py:62
  154.8 6.3 collective-permute-start
  166.2 6.3 collective-permute-start
  222.3 6.3 collective-permute-start.2
  244.9 6.3 collective-permute-start.2
  267.3 6.3 collective-permute-start.2
  301.1 6.3 collective-permute-start.6
  312.8 8.1 %collective-permute-start.6 = (f32[16,1,128]{2,1,0:T(1,128)S(1)}, f32[16,1,128]{2,1,0:T(1,128)S(1)}, u32[]{:S(2)}, u32[]{:S(2)}) collective-permute-start(f32[16,1,128]{2,1,0:T(1,128)S(1)} %slice.355), channel_id=1, source_target_pairs={{0,1},{1,2},{2,3},{3,4},{4,5},{5,6},{6,7},{7,8},{8,9},{9,10},{10,1... | collective-permute-start | bytes 24584 | tf_op jit(solution)/shard_map/while/body/eval_jaxpr/ppermute | solution.py:26
  326.3 7.8 %collective-permute-start.6 = (f32[16,1,128]{2,1,0:T(1,128)S(1)}, f32[16,1,128]{2,1,0:T(1,128)S(1)}, u32[]{:S(2)}, u32[]{:S(2)}) collective-permute-start(f32[16,1,128]{2,1,0:T(1,128)S(1)} %slice.355), channel_id=1, source_target_pairs={{0,1},{1,2},{2,3},{3,4},{4,5},{5,6},{6,7},{7,8},{8,9},{9,10},{10,1... | collective-permute-start | bytes 24584 | tf_op jit(solution)/shard_map/while/body/eval_jaxpr/ppermute | solution.py:26
  339.1 8.6 %collective-permute-start.6 = (f32[16,1,128]{2,1,0:T(1,128)S(1)}, f32[16,1,128]{2,1,0:T(1,128)S(1)}, u32[]{:S(2)}, u32[]{:S(2)}) collective-permute-start(f32[16,1,128]{2,1,0:T(1,128)S(1)} %slice.355), channel_id=1, source_target_pairs={{0,1},{1,2},{2,3},{3,4},{4,5},{5,6},{6,7},{7,8},{8,9},{9,10},{10,1... | collective-permute-start | bytes 24584 | tf_op jit(solution)/shard_map/while/body/eval_jaxpr/ppermute | solution.py:26
  352.6 8.1 %collective-permute-start.6 = (f32[16,1,128]{2,1,0:T(1,128)S(1)}, f32[16,1,128]{2,1,0:T(1,128)S(1)}, u32[]{:S(2)}, u32[]{:S(2)}) collective-permute-start(f32[16,1,128]{2,1,0:T(1,128)S(1)} %slice.355), channel_id=1, source_target_pairs={{0,1},{1,2},{2,3},{3,4},{4,5},{5,6},{6,7},{7,8},{8,9},{9,10},{10,1... | collective-permute-start | bytes 24584 | tf_op jit(solution)/shard_map/while/body/eval_jaxpr/ppermute | solution.py:26
  365.9 8.4 %collective-permute-start.6 = (f32[16,1,128]{2,1,0:T(1,128)S(1)}, f32[16,1,128]{2,1,0:T(1,128)S(1)}, u32[]{:S(2)}, u32[]{:S(2)}) collective-permute-start(f32[16,1,128]{2,1,0:T(1,128)S(1)} %slice.355), channel_id=1, source_target_pairs={{0,1},{1,2},{2,3},{3,4},{4,5},{5,6},{6,7},{7,8},{8,9},{9,10},{10,1... | collective-permute-start | bytes 24584 | tf_op jit(solution)/shard_map/while/body/eval_jaxpr/ppermute | solution.py:26
  379.5 8.0 %collective-permute-start.6 = (f32[16,1,128]{2,1,0:T(1,128)S(1)}, f32[16,1,128]{2,1,0:T(1,128)S(1)}, u32[]{:S(2)}, u32[]{:S(2)}) collective-permute-start(f32[16,1,128]{2,1,0:T(1,128)S(1)} %slice.355), channel_id=1, source_target_pairs={{0,1},{1,2},{2,3},{3,4},{4,5},{5,6},{6,7},{7,8},{8,9},{9,10},{10,1... | collective-permute-start | bytes 24584 | tf_op jit(solution)/shard_map/while/body/eval_jaxpr/ppermute | solution.py:26
  392.7 8.0 %collective-permute-start.6 = (f32[16,1,128]{2,1,0:T(1,128)S(1)}, f32[16,1,128]{2,1,0:T(1,128)S(1)}, u32[]{:S(2)}, u32[]{:S(2)}) collective-permute-start(f32[16,1,128]{2,1,0:T(1,128)S(1)} %slice.355), channel_id=1, source_target_pairs={{0,1},{1,2},{2,3},{3,4},{4,5},{5,6},{6,7},{7,8},{8,9},{9,10},{10,1... | collective-permute-start | bytes 24584 | tf_op jit(solution)/shard_map/while/body/eval_jaxpr/ppermute | solution.py:26
  406.0 8.4 %collective-permute-start.4 = (f32[16,1,128]{2,1,0:T(1,128)S(1)}, f32[16,1,128]{2,1,0:T(1,128)S(1)}, u32[]{:S(2)}, u32[]{:S(2)}) collective-permute-start(f32[16,1,128]{2,1,0:T(1,128)S(1)} %slice.351), channel_id=1, source_target_pairs={{0,1},{1,2},{2,3},{3,4},{4,5},{5,6},{6,7},{7,8},{8,9},{9,10},{10,1... | collective-permute-start | bytes 24584 | tf_op jit(solution)/shard_map/while/body/eval_jaxpr/ppermute | solution.py:26
  419.6 8.1 %collective-permute-start.4 = (f32[16,1,128]{2,1,0:T(1,128)S(1)}, f32[16,1,128]{2,1,0:T(1,128)S(1)}, u32[]{:S(2)}, u32[]{:S(2)}) collective-permute-start(f32[16,1,128]{2,1,0:T(1,128)S(1)} %slice.351), channel_id=1, source_target_pairs={{0,1},{1,2},{2,3},{3,4},{4,5},{5,6},{6,7},{7,8},{8,9},{9,10},{10,1... | collective-permute-start | bytes 24584 | tf_op jit(solution)/shard_map/while/body/eval_jaxpr/ppermute | solution.py:26
  432.8 8.4 %collective-permute-start.4 = (f32[16,1,128]{2,1,0:T(1,128)S(1)}, f32[16,1,128]{2,1,0:T(1,128)S(1)}, u32[]{:S(2)}, u32[]{:S(2)}) collective-permute-start(f32[16,1,128]{2,1,0:T(1,128)S(1)} %slice.351), channel_id=1, source_target_pairs={{0,1},{1,2},{2,3},{3,4},{4,5},{5,6},{6,7},{7,8},{8,9},{9,10},{10,1... | collective-permute-start | bytes 24584 | tf_op jit(solution)/shard_map/while/body/eval_jaxpr/ppermute | solution.py:26
  446.1 8.1 %collective-permute-start.4 = (f32[16,1,128]{2,1,0:T(1,128)S(1)}, f32[16,1,128]{2,1,0:T(1,128)S(1)}, u32[]{:S(2)}, u32[]{:S(2)}) collective-permute-start(f32[16,1,128]{2,1,0:T(1,128)S(1)} %slice.351), channel_id=1, source_target_pairs={{0,1},{1,2},{2,3},{3,4},{4,5},{5,6},{6,7},{7,8},{8,9},{9,10},{10,1... | collective-permute-start | bytes 24584 | tf_op jit(solution)/shard_map/while/body/eval_jaxpr/ppermute | solution.py:26
  459.4 8.4 %collective-permute-start.4 = (f32[16,1,128]{2,1,0:T(1,128)S(1)}, f32[16,1,128]{2,1,0:T(1,128)S(1)}, u32[]{:S(2)}, u32[]{:S(2)}) collective-permute-start(f32[16,1,128]{2,1,0:T(1,128)S(1)} %slice.351), channel_id=1, source_target_pairs={{0,1},{1,2},{2,3},{3,4},{4,5},{5,6},{6,7},{7,8},{8,9},{9,10},{10,1... | collective-permute-start | bytes 24584 | tf_op jit(solution)/shard_map/while/body/eval_jaxpr/ppermute | solution.py:26
  473.0 8.0 %collective-permute-start.4 = (f32[16,1,128]{2,1,0:T(1,128)S(1)}, f32[16,1,128]{2,1,0:T(1,128)S(1)}, u32[]{:S(2)}, u32[]{:S(2)}) collective-permute-start(f32[16,1,128]{2,1,0:T(1,128)S(1)} %slice.351), channel_id=1, source_target_pairs={{0,1},{1,2},{2,3},{3,4},{4,5},{5,6},{6,7},{7,8},{8,9},{9,10},{10,1... | collective-permute-start | bytes 24584 | tf_op jit(solution)/shard_map/while/body/eval_jaxpr/ppermute | solution.py:26
  486.2 8.1 %collective-permute-start.4 = (f32[16,1,128]{2,1,0:T(1,128)S(1)}, f32[16,1,128]{2,1,0:T(1,128)S(1)}, u32[]{:S(2)}, u32[]{:S(2)}) collective-permute-start(f32[16,1,128]{2,1,0:T(1,128)S(1)} %slice.351), channel_id=1, source_target_pairs={{0,1},{1,2},{2,3},{3,4},{4,5},{5,6},{6,7},{7,8},{8,9},{9,10},{10,1... | collective-permute-start | bytes 24584 | tf_op jit(solution)/shard_map/while/body/eval_jaxpr/ppermute | solution.py:26
  500.1 7.8 %collective-permute-start.4 = (f32[16,1,128]{2,1,0:T(1,128)S(1)}, f32[16,1,128]{2,1,0:T(1,128)S(1)}, u32[]{:S(2)}, u32[]{:S(2)}) collective-permute-start(f32[16,1,128]{2,1,0:T(1,128)S(1)} %slice.351), channel_id=1, source_target_pairs={{0,1},{1,2},{2,3},{3,4},{4,5},{5,6},{6,7},{7,8},{8,9},{9,10},{10,1... | collective-permute-start | bytes 24584 | tf_op jit(solution)/shard_map/while/body/eval_jaxpr/ppermute | solution.py:26
  515.5 81.0 %all-to-all-start.3 = ((f32[16,512,128]{2,0,1:T(8,128)}), f32[16,512,128]{2,0,1:T(8,128)}, u32[]{:S(2)}, u32[]{:S(2)}) async-start(f32[16,512,128]{2,0,1:T(8,128)} %bitcast.129), calls=%async_computation.3 | async-start | bytes 8388608 | tf_op jit(solution)/shard_map/all_to_all | solution.py:18
  (51 other events, 436.1 us)
Sparse Core Ops, SparseCore 0:
  45.7 76.5 all-gather.2
